TPU v7x, 128 devices: a whole 4x4x4 slice. The times are simulated.
128 devices in a mesh: blk: 8 (over x, y_hi), sub: 2 (over y_lo), feat: 8 (over z, core).
Axes of the slice: x: 4, y: 4 (y_hi: 2, y_lo: 2; y = y_hi * 2 + y_lo), z: 4, core: 2. Of those that a mesh axis runs over, the one named last changes fastest.
Arguments:
- sources: bfloat16 [131072, 1024], P(('blk', 'sub'), 'feat'), may hold values from -6 to 6
- adjacency: bfloat16 [16, 16, 32, 128, 128], P(('blk', 'sub')), may hold values from -0.15625 to 0.15625
- target_block: int32 [16, 16, 32], P(('blk', 'sub')), may hold values from 0 to 7
- source_block: int32 [16, 16, 32], P(('blk', 'sub')), may hold values from 0 to 63
- slot_counts: int32 [16, 16], P(('blk', 'sub')), may hold values from 1 to 32, as said below
- weight: bfloat16 [1024, 1024], P(None, 'feat'), may hold values from -0.1875 to 0.1875
Outputs:
- activated: bfloat16 [16384, 1024], P(('blk', 'sub'), 'feat')
Inputs may be any that keep to these rules, and one draw needn't show every extreme that they name: Every stripe and piece uses its first slot_counts slots; in every draw some stripe and piece uses all 32.
All inputs are finite; a program needn't handle non-finite values.
Results may differ from a plain program's by a relative error of at most 0.0049.
Values may be sent and summed in bfloat16 or wider, within the bound.
A program may use at most 192 MiB of HBM per device.

v0:
```python
import jax
import jax.numpy as jnp
from jax import lax
from jax.sharding import PartitionSpec as P

BLOCK = 128
TGT_DEV = 1024


def local_products(adj_group, rows_group, cols_group, counts_group, blocks):
    slot_total = adj_group.shape[1]
    block_total = blocks.shape[0]
    target_total = TGT_DEV // BLOCK
    feat_width = blocks.shape[2]

    def one_piece(adj_piece, rows_piece, cols_piece, count_piece):
        source_hot = (
            cols_piece[:, None] == jnp.arange(block_total, dtype=jnp.int32)[None, :]
        ).astype(jnp.bfloat16)
        selected = jnp.einsum(
            "sk,kif->sif", source_hot, blocks, preferred_element_type=jnp.float32
        ).astype(jnp.bfloat16)
        product = jnp.einsum(
            "sij,sjf->sif", adj_piece, selected, preferred_element_type=jnp.float32
        )
        live_slots = jnp.arange(slot_total, dtype=jnp.int32) < count_piece
        target_hot = (
            (jnp.arange(target_total, dtype=jnp.int32)[:, None] == rows_piece[None, :])
            & live_slots[None, :]
        ).astype(jnp.float32)
        summed = jnp.einsum("ts,sif->tif", target_hot, product, precision=lax.Precision.HIGHEST)
        return summed.reshape(TGT_DEV, feat_width)

    return jax.vmap(one_piece)(adj_group, rows_group, cols_group, counts_group)


def body(sources, adjacency, target_block, source_block, slot_counts, weight):
    feat_width = sources.shape[1]
    blocks = sources.reshape(sources.shape[0] // BLOCK, BLOCK, feat_width)
    adj_local = adjacency[0]
    target_local = target_block[0]
    source_local = source_block[0]
    count_local = slot_counts[0]
    piece_terms = local_products(adj_local, target_local, source_local, count_local, blocks)
    summed = lax.psum_scatter(
        piece_terms.reshape(TGT_DEV * lax.axis_size(("blk", "sub")), feat_width),
        ("blk", "sub"),
        scatter_dimension=0,
        tiled=True,
    )
    hidden = summed.astype(jnp.bfloat16)
    projected = jnp.dot(
        lax.all_gather(hidden, "feat", axis=1, tiled=True),
        weight,
        preferred_element_type=jnp.float32,
    )
    return jax.nn.relu(projected).astype(jnp.bfloat16)


def solution(mesh):
    return jax.shard_map(
        body,
        mesh=mesh,
        in_specs=(
            P(("blk", "sub"), "feat"),
            P(("blk", "sub"), None, None, None, None),
            P(("blk", "sub"), None, None),
            P(("blk", "sub"), None, None),
            P(("blk", "sub"), None),
            P(None, "feat"),
        ),
        out_specs=P(("blk", "sub"), "feat"),
        check_vma=False,
    )
```

profile of v0, /device:TPU:1, one launch (start us, length us, event | category | flops | bytes accessed | tf_op | source)
XLA Modules:
  0.0 231.1 jit_solution(8355572814757949704)
XLA Ops:
  6.5 0.0 copy-start
  6.5 0.0 reduce-scatter.2.cloned.1.call-start
  6.5 1.6 copy-done
  8.1 9.7 %fusion.4 = bf16[16,32,128,128]{3,1,2,0:T(8,128)(2,1)} fusion(bf16[64,128,128,1]{2,1,0,3:T(8,128)(2,1)S(1)} %bitcast.25, s32[16,32]{1,0:T(8,128)} %bitcast.27), kind=kOutput, calls=%fused_computation.5 | convolution fusion | flops 1073774592 | bytes 18876416 | tf_op jit(solution)/shard_map/vmap(sk,kif->sif)/dot_general | solution.py:20
  17.9 23.3 %fusion.2 = f32[16,32,128,128]{3,2,1,0:T(8,128)} fusion(bf16[16,32,128,128]{3,1,2,0:T(8,128)(2,1)} %fusion.4, bf16[1,16,32,128,128]{4,3,2,1,0:T(8,128)(2,1)} %param.7), kind=kOutput, calls=%fused_computation.3 | convolution fusion | flops 2147483648 | bytes 67108864 | tf_op jit(solution)/shard_map/vmap(sij,sjf->sif)/dot_general | solution.py:23
  41.2 0.0 copy-start.3
  41.2 0.0 copy-start.2
  41.2 34.6 %copy.11 = f32[16,32,128,128]{2,1,3,0:T(8,128)} copy(f32[16,32,128,128]{3,2,1,0:T(8,128)} %fusion.2) | data formatting | bytes 67108864 | tf_op jit(solution)/shard_map/vmap(sij,sjf->sif)/dot_general | solution.py:23
  75.8 0.0 copy-done.3
  75.8 0.1 iota_compare_fusion.2
  75.8 0.0 copy-done.2
  75.8 0.0 copy-start.1
  75.8 19.4 %fusion = f32[16,8,128,128]{3,1,2,0:T(8,128)} fusion(f32[16,32,128,128]{2,1,3,0:T(8,128)} %copy.11, s32[16,32]{1,0:T(8,128)S(1)} %bitcast.28, pred[16,32]{1,0:T(8,128)(4,1)S(1)} %iota_compare_fusion.2), kind=kOutput, calls=%fused_computation | convolution fusion | flops 805314560 | bytes 41945600 | tf_op jit(solution)/shard_map/vmap(ts,sif->tif)/dot_general | solution.py:31
  95.3 0.0 copy-start.4
  95.3 8.1 %copy.7 = f32[16,8,128,128]{3,2,1,0:T(8,128)} copy(f32[16,8,128,128]{3,1,2,0:T(8,128)} %fusion) | data formatting | bytes 16777216 | tf_op jit(solution)/shard_map/vmap(ts,sif->tif)/dot_general | solution.py:31
  103.4 0.0 reduce-scatter.2.cloned.1.call-update
  103.4 0.0 all-gather.2.cloned.1.call-start
  103.5 87.6 %reduce-scatter.2.cloned.1.call-done = f32[1024,128]{1,0:T(8,128)} async-done(((f32[16384,128]{1,0:T(8,128)}), f32[1024,128]{1,0:T(8,128)}) %reduce-scatter.2.cloned.1.call-update) | async-done | bytes 524304 | tf_op jit(solution)/shard_map/reduce_scatter | solution.py:45
  191.0 1.8 convert_element_type.12
  192.8 0.0 all-gather.2.cloned.1.call-update
  192.8 28.5 %all-gather.2.cloned.1.call-done = bf16[1024,1024]{1,0:T(8,128)(2,1)} async-done(((bf16[1024,128]{1,0:T(8,128)(2,1)}), bf16[1024,1024]{1,0:T(8,128)(2,1)}) %all-gather.2.cloned.1.call-update) | async-done | bytes 2097168 | tf_op jit(solution)/shard_map/all_gather | solution.py:53
  221.3 0.0 copy-done.4
  221.3 3.0 %fusion.6 = bf16[1024,128]{1,0:T(8,128)(2,1)} fusion(bf16[1024,1024]{1,0:T(8,128)(2,1)} %all-gather.2.cloned.1.call-done, bf16[1024,128]{1,0:T(8,128)(2,1)S(1)} %copy-done.4), kind=kOutput, calls=%fused_computation.8 | convolution fusion | flops 268697600 | bytes 2621440 | tf_op jit(solution)/shard_map/dot_general | solution.py:52
  224.3 0.0 copy-done.1
Async XLA Ops:
  6.5 1.6 copy-start
  6.5 184.5 %reduce-scatter.2.cloned.1.call-start = ((), (), s32[]{:S(2)}) async-start(), calls=%async_computation.1 | async-start | bytes 8912896 | tf_op jit(solution)/shard_map/reduce_scatter | solution.py:45
  41.2 34.6 %copy-start.3 = (s32[1,16]{1,0:T(1,128)S(1)}, s32[1,16]{1,0:T(1,128)}, u32[]{:S(2)}) copy-start(s32[1,16]{1,0:T(1,128)} %param.10) | copy-start | bytes 196
  41.2 34.7 %copy-start.2 = (s32[1,16,32]{2,1,0:T(8,128)S(1)}, s32[1,16,32]{2,1,0:T(8,128)}, u32[]{:S(2)}) copy-start(s32[1,16,32]{2,1,0:T(8,128)} %param.8) | copy-start | bytes 6148
  75.8 148.5 %copy-start.1 = (bf16[8192,128]{1,0:T(8,128)(2,1)S(1)}, bf16[8192,128]{1,0:T(8,128)(2,1)}, u32[]{:S(2)}) copy-start(bf16[8192,128]{1,0:T(8,128)(2,1)} %param.6) | copy-start | bytes 6291460
  95.3 126.0 %copy-start.4 = (bf16[1024,128]{1,0:T(8,128)(2,1)S(1)}, bf16[1024,128]{1,0:T(8,128)(2,1)}, u32[]{:S(2)}) copy-start(bf16[1024,128]{1,0:T(8,128)(2,1)} %param.11) | copy-start | bytes 786436
  103.4 117.9 %all-gather.2.cloned.1.call-start = ((), (), s32[]{:S(2)}) async-start(), calls=%async_computation.2 | async-start | bytes 2359296 | tf_op jit(solution)/shard_map/all_gather | solution.py:53
Sparse Core Ops, SparseCore 0:
  103.6 87.4 reduce-scatter.1
  193.0 28.2 all-gather.1
where the time goes:
time: 232 us; the launch traced here: 231 us
  waiting for transfers between devices  116 us (50%)
  matrix products  55.5 us (24%)
  local copies, waits for them, and re-layouts  44.3 us (19%)
  between operations  13.4 us (6%)
    reduce_scatter x1, waiting for transfers between devices, body(): lax.psum_scatter(piece_terms.reshape(TGT_DEV * lax.axis_size(('blk', 'sub...  87.6 us
    dot_general x1, local copies, waits for them, and re-layouts, one_piece(): jnp.einsum('sij,sjf->sif', adj_piece, selected, preferred_element_type=jn...  34.6 us
    all_gather x1, waiting for transfers between devices, body(): lax.all_gather(hidden, 'feat', axis=1, tiled=True)  28.5 us
    dot_general x1, matrix products, one_piece(): jnp.einsum('sij,sjf->sif', adj_piece, selected, preferred_element_type=jn...  23.3 us
    dot_general x1, matrix products, one_piece(): jnp.einsum('ts,sif->tif', target_hot, product, precision=lax.Precision.HI...  19.4 us
    dot_general x1, matrix products, one_piece(): jnp.einsum('sk,kif->sif', source_hot, blocks, preferred_element_type=jnp....  9.75 us
    dot_general x1, local copies, waits for them, and re-layouts, one_piece(): jnp.einsum('ts,sif->tif', target_hot, product, precision=lax.Precision.HI...  8.13 us
  transfers between devices with their start and end apart: 2, of which 2 were waited for; matrix products, arithmetic and copies ran while one was open for 0% of the time, Pallas kernels for 0%

commit v1 on v0

v1 whole, which is shorter than its diff:
```python
import functools

import jax
import jax.numpy as jnp
from jax import lax
from jax.experimental import pallas as pl
from jax.experimental.pallas import tpu as pltpu
from jax.sharding import PartitionSpec as P

BLOCK = 128
TGT_DEV = 1024
UNROLL = 4


def aggregate_kernel(target_ref, source_ref, count_ref, adj_ref, blocks_ref, out_ref, total_ref):
    piece = pl.program_id(0)
    block_total = TGT_DEV // BLOCK
    count = count_ref[piece]
    total_ref[...] = jnp.zeros_like(total_ref)

    def group(step, carry):
        products = []
        for u in range(UNROLL):
            slot = step * UNROLL + u
            products.append(
                jnp.dot(
                    adj_ref[0, slot],
                    blocks_ref[source_ref[piece, slot]],
                    preferred_element_type=jnp.float32,
                )
            )
        for u in range(UNROLL):
            slot = step * UNROLL + u
            row = jnp.where(slot < count, target_ref[piece, slot], block_total)
            total_ref[row] += products[u]
        return carry

    lax.fori_loop(0, (count + UNROLL - 1) // UNROLL, group, 0)
    out_ref[0] = total_ref[:block_total].reshape(TGT_DEV, BLOCK)


def aggregate(target, source, count, adj, blocks):
    pieces, slots = target.shape
    return pl.pallas_call(
        aggregate_kernel,
        out_shape=jax.ShapeDtypeStruct((pieces, TGT_DEV, blocks.shape[2]), jnp.float32),
        grid_spec=pltpu.PrefetchScalarGridSpec(
            num_scalar_prefetch=3,
            grid=(pieces,),
            in_specs=[
                pl.BlockSpec((1, slots, BLOCK, BLOCK), lambda p, *_: (p, 0, 0, 0)),
                pl.BlockSpec(memory_space=pltpu.VMEM),
            ],
            out_specs=pl.BlockSpec((1, TGT_DEV, blocks.shape[2]), lambda p, *_: (p, 0, 0)),
            scratch_shapes=[pltpu.VMEM((TGT_DEV // BLOCK + 1, BLOCK, blocks.shape[2]), jnp.float32)],
        ),
        compiler_params=pltpu.CompilerParams(vmem_limit_bytes=32 << 20),
        name="aggregate",
    )(target, source, count, adj, blocks)


def body(sources, adjacency, target_block, source_block, slot_counts, weight):
    feat_width = sources.shape[1]
    blocks = sources.reshape(sources.shape[0] // BLOCK, BLOCK, feat_width)
    piece_terms = aggregate(target_block[0], source_block[0], slot_counts[0], adjacency[0], blocks)
    summed = lax.psum_scatter(
        piece_terms.reshape(TGT_DEV * lax.axis_size(("blk", "sub")), feat_width),
        ("blk", "sub"),
        scatter_dimension=0,
        tiled=True,
    )
    hidden = summed.astype(jnp.bfloat16)
    projected = jnp.dot(
        lax.all_gather(hidden, "feat", axis=1, tiled=True),
        weight,
        preferred_element_type=jnp.float32,
    )
    return jax.nn.relu(projected).astype(jnp.bfloat16)


def solution(mesh):
    return jax.shard_map(
        body,
        mesh=mesh,
        in_specs=(
            P(("blk", "sub"), "feat"),
            P(("blk", "sub"), None, None, None, None),
            P(("blk", "sub"), None, None),
            P(("blk", "sub"), None, None),
            P(("blk", "sub"), None),
            P(None, "feat"),
        ),
        out_specs=P(("blk", "sub"), "feat"),
        check_vma=False,
    )
```

time: 232 us -> 164 us (0.71)
  matrix products: 55.5 us -> 3 us
  local copies, waits for them, and re-layouts: 44.3 us -> 6.91 us
  Pallas kernels: 0 us -> 14.7 us
  waiting for transfers between devices: 116 us -> 123 us
    dot_general x3 -> x0, matrix products: 52.5 us -> none  [the longest x1 23.3 us: one_piece(): jnp.einsum('sij,sjf->sif', adj_piece, selected, preferred_element_type=jn...]
    dot_general x2 -> x0, local copies, waits for them, and re-layouts: 42.7 us -> none  [the longest x1 34.6 us: one_piece(): jnp.einsum('sij,sjf->sif', adj_piece, selected, preferred_element_type=jn...]
    pallas_call x0 -> x1, Pallas kernels: none -> 14.7 us  [aggregate(): pl.pallas_call(aggregate_kernel, out_shape=jax.ShapeDtypeStruct((pieces,...]
    reduce_scatter x1, waiting for transfers between devices: 87.6 us -> 94.9 us  [body(): lax.psum_scatter(piece_terms.reshape(TGT_DEV * lax.axis_size(('blk', 'sub...]
    unnamed x10 -> x12, local copies, waits for them, and re-layouts: 1.6 us -> 6.91 us
where the time goes in v1:
time: 164 us; the launch traced here: 163 us
  waiting for transfers between devices  123 us (75%)
  Pallas kernels  14.7 us (9%)
  between operations  13.4 us (8%)
  local copies, waits for them, and re-layouts  6.91 us (4%)
  matrix products  3 us (2%)
  other arithmetic  1.77 us (1%)
    reduce_scatter x1, waiting for transfers between devices, body(): lax.psum_scatter(piece_terms.reshape(TGT_DEV * lax.axis_size(('blk', 'sub...  94.9 us
    all_gather x1, waiting for transfers between devices, body(): lax.all_gather(hidden, 'feat', axis=1, tiled=True)  28.3 us
    pallas_call x1, Pallas kernels, aggregate(): pl.pallas_call(aggregate_kernel, out_shape=jax.ShapeDtypeStruct((pieces,...  14.7 us
    unnamed x12, local copies, waits for them, and re-layouts  6.91 us
  transfers between devices with their start and end apart: 2, of which 2 were waited for; matrix products, arithmetic and copies ran while one was open for 0% of the time, Pallas kernels for 0%

profile of v1, /device:TPU:1, one launch (start us, length us, event | category | flops | bytes accessed | tf_op | source)
XLA Modules:
  0.0 163.2 jit_solution(4366326646618564410)
XLA Ops:
  6.5 0.0 copy-start
  6.5 0.0 reduce-scatter.2.cloned.1.call-start
  6.5 0.0 copy-start.2
  6.5 1.6 %copy-done.2 = bf16[8192,128]{1,0:T(8,128)(2,1)S(1)} copy-done((bf16[8192,128]{1,0:T(8,128)(2,1)S(1)}, bf16[8192,128]{1,0:T(8,128)(2,1)}, u32[]{:S(2)}) %copy-start.2) | copy-done | bytes 2097176
  8.2 0.0 copy-start.3
  8.2 0.7 copy-done.3
  8.9 0.0 copy-start.4
  8.9 0.7 copy-done.4
  9.6 0.0 copy-start.5
  9.6 0.7 copy-done.5
  10.2 14.7 %aggregate.1 = f32[16,1024,128]{2,1,0:T(8,128)S(1)} custom-call(s32[16,32]{1,0:T(8,128)S(1)} %bitcast.10, s32[16,32]{1,0:T(8,128)S(1)} %bitcast.11, s32[16]{0:T(128)S(1)} %bitcast.12, bf16[16,32,128,128]{3,2,1,0:T(8,128)(2,1)} %bitcast.13, bf16[64,128,128]{2,1,0:T(8,128)(2,1)S(1)} %bitcast.9), custom_call_target="tpu_custom_call" | custom-call | tf_op jit(solution)/shard_map/aggregate/pallas_call | solution.py:44
  25.0 0.0 copy-start.1
  25.0 3.2 %copy-done.1 = f32[16,1024,128]{2,1,0:T(8,128)} copy-done((f32[16,1024,128]{2,1,0:T(8,128)}, f32[16,1024,128]{2,1,0:T(8,128)S(1)}, u32[]{:S(2)}) %copy-start.1) | copy-done | bytes 8388632
  28.2 0.0 reduce-scatter.2.cloned.1.call-update
  28.2 0.0 all-gather.2.cloned.1.call-start
  28.3 94.9 %reduce-scatter.2.cloned.1.call-done = f32[1024,128]{1,0:T(8,128)} async-done(((f32[16384,128]{1,0:T(8,128)}), f32[1024,128]{1,0:T(8,128)}) %reduce-scatter.2.cloned.1.call-update) | async-done | bytes 524304 | tf_op jit(solution)/shard_map/reduce_scatter | solution.py:66
  123.2 1.8 %convert_element_type.6 = bf16[1024,128]{1,0:T(8,128)(2,1)} convert(f32[1024,128]{1,0:T(8,128)} %reduce-scatter.2.cloned.1.call-done) | non-fusion elementwise | flops 131072 | bytes 786432 | tf_op jit(solution)/shard_map/convert_element_type | solution.py:72
  125.0 0.0 all-gather.2.cloned.1.call-update
  125.0 28.3 %all-gather.2.cloned.1.call-done = bf16[1024,1024]{1,0:T(8,128)(2,1)} async-done(((bf16[1024,128]{1,0:T(8,128)(2,1)}), bf16[1024,1024]{1,0:T(8,128)(2,1)}) %all-gather.2.cloned.1.call-update) | async-done | bytes 2097168 | tf_op jit(solution)/shard_map/all_gather | solution.py:74
  153.3 0.0 copy-done
  153.3 3.0 %fusion = bf16[1024,128]{1,0:T(8,128)(2,1)} fusion(bf16[1024,1024]{1,0:T(8,128)(2,1)} %all-gather.2.cloned.1.call-done, bf16[1024,128]{1,0:T(8,128)(2,1)S(1)} %copy-done), kind=kOutput, calls=%fused_computation.1 | convolution fusion | flops 268697600 | bytes 2621440 | tf_op jit(solution)/shard_map/dot_general | solution.py:73
Async XLA Ops:
  6.5 146.8 %copy-start = (bf16[1024,128]{1,0:T(8,128)(2,1)S(1)}, bf16[1024,128]{1,0:T(8,128)(2,1)}, u32[]{:S(2)}) copy-start(bf16[1024,128]{1,0:T(8,128)(2,1)} %param.11) | copy-start | bytes 786436
  6.5 116.7 %reduce-scatter.2.cloned.1.call-start = ((), (), s32[]{:S(2)}) async-start(), calls=%async_computation.1 | async-start | bytes 8912896 | tf_op jit(solution)/shard_map/reduce_scatter | solution.py:66
  6.5 1.6 %copy-start.2 = (bf16[8192,128]{1,0:T(8,128)(2,1)S(1)}, bf16[8192,128]{1,0:T(8,128)(2,1)}, u32[]{:S(2)}) copy-start(bf16[8192,128]{1,0:T(8,128)(2,1)} %param.6) | copy-start | bytes 6291460
  8.2 0.7 copy-start.3
  8.9 0.7 copy-start.4
  9.6 0.7 copy-start.5
  25.0 3.2 %copy-start.1 = (f32[16,1024,128]{2,1,0:T(8,128)}, f32[16,1024,128]{2,1,0:T(8,128)S(1)}, u32[]{:S(2)}) copy-start(f32[16,1024,128]{2,1,0:T(8,128)S(1)} %aggregate.1) | copy-start | bytes 25165828
  28.2 125.1 %all-gather.2.cloned.1.call-start = ((), (), s32[]{:S(2)}) async-start(), calls=%async_computation.2 | async-start | bytes 2359296 | tf_op jit(solution)/shard_map/all_gather | solution.py:74
Sparse Core Ops, SparseCore 0:
  28.3 94.8 reduce-scatter.1
  125.1 28.1 all-gather.1

commit v2 on v1

v2 whole, which is shorter than its diff:
```python
import jax
import jax.numpy as jnp
from jax import lax
from jax.experimental import pallas as pl
from jax.experimental.pallas import tpu as pltpu
from jax.sharding import PartitionSpec as P

BLOCK = 128
TGT_DEV = 1024
UNROLL = 8
RING = 4
CHUNKS = (128,) * 8
MESH = pl.DeviceIdType.MESH


def aggregate_kernel(core_ref, target_ref, source_ref, count_ref, adj_ref, blocks_ref, out_ref, total_ref):
    piece = pl.program_id(0)
    block_total = TGT_DEV // BLOCK
    count = count_ref[piece]
    total_ref[...] = jnp.zeros_like(total_ref)

    def group(step, carry):
        products = []
        for u in range(UNROLL):
            slot = step * UNROLL + u
            products.append(
                jnp.dot(
                    adj_ref[0, slot],
                    blocks_ref[source_ref[piece, slot]],
                    preferred_element_type=jnp.float32,
                )
            )
        for u in range(UNROLL):
            slot = step * UNROLL + u
            row = jnp.where(slot < count, target_ref[piece, slot], block_total)
            total_ref[row] += products[u]
        return carry

    lax.fori_loop(0, (count + UNROLL - 1) // UNROLL, group, 0)
    out_ref[0] = total_ref[:block_total].reshape(TGT_DEV, BLOCK).astype(out_ref.dtype)


def aggregate(core, target, source, count, adj, blocks):
    pieces, slots = target.shape

    def placed(p, core_ref, *_):
        return ((p // RING) * (RING - core_ref[0] * (RING - 1)) + (p % RING) * (1 + core_ref[0] * (RING - 1)), 0, 0)

    return pl.pallas_call(
        aggregate_kernel,
        out_shape=jax.ShapeDtypeStruct((pieces, TGT_DEV, blocks.shape[2]), jnp.bfloat16),
        grid_spec=pltpu.PrefetchScalarGridSpec(
            num_scalar_prefetch=4,
            grid=(pieces,),
            in_specs=[
                pl.BlockSpec((1, slots, BLOCK, BLOCK), lambda p, *_: (p, 0, 0, 0)),
                pl.BlockSpec(memory_space=pltpu.VMEM),
            ],
            out_specs=pl.BlockSpec((1, TGT_DEV, blocks.shape[2]), placed),
            scratch_shapes=[pltpu.VMEM((TGT_DEV // BLOCK + 1, BLOCK, blocks.shape[2]), jnp.float32)],
        ),
        compiler_params=pltpu.CompilerParams(vmem_limit_bytes=40 << 20),
        name="aggregate",
    )(core, target, source, count, adj, blocks)


F1, C1, P1, F2, C2, P2, Z1, Z2, OWN, FWD1, FWD2 = range(0, 22, 2)
KINDS = 22


def exchange_kernel(
    part, weight_ref, out_ref, got1, mix1, row32, row16, got2, mix2, hidden, send_sems, recv_sems
):
    blk, sub, feat = lax.axis_index("blk"), lax.axis_index("sub"), lax.axis_index("feat")
    x, y = blk // 2, (blk % 2) * 2 + sub
    z, core = feat // 2, feat % 2
    ia = x * (1 - core) + y * core
    ib = y * (1 - core) + x * core

    def at(ja, jb, jz, jcore):
        px = ja * (1 - core) + jb * core
        py = jb * (1 - core) + ja * core
        return (px * 2 + py // 2, py % 2, jz * 2 + jcore)

    step = (1, RING - 1)
    near_a = [(ia + s) % RING for s in step]
    near_b = [(ib + s) % RING for s in step]
    near_z = [(z + s) % RING for s in step]
    dev_a = [at(j, ib, z, core) for j in near_a]
    dev_b = [at(ia, j, z, core) for j in near_b]
    dev_z = [at(ia, ib, j, core) for j in near_z]
    mate = (blk, sub, z * 2 + 1 - core)
    far_a, far_b = (ia + 2) % RING, (ib + 2) % RING

    barrier = pltpu.get_barrier_semaphore()
    everyone = dev_a + dev_b + dev_z + [mate]
    for device in everyone:
        pl.semaphore_signal(barrier, inc=1, device_id=device, device_id_type=MESH)
    pl.semaphore_wait(barrier, len(everyone))

    starts = [sum(CHUNKS[:c]) for c in range(len(CHUNKS))]

    def rows(c, half=None):
        n = CHUNKS[c]
        if half is None:
            return pl.ds(starts[c], n)
        return pl.ds(starts[c] + half * (n // 2), n // 2)

    def packed(c):
        return pl.ds(starts[c] // 2, CHUNKS[c] // 2)

    def copy(kind, c, src, dst, device):
        return pltpu.make_async_remote_copy(
            src_ref=src,
            dst_ref=dst,
            send_sem=send_sems.at[kind, c],
            recv_sem=recv_sems.at[kind, c],
            device_id=device,
            device_id_type=MESH,
        )

    def first(kind, c, d):
        if kind == F1:
            src = part.at[far_a, :, rows(c, d)]
        elif kind == P1:
            src = part.at[near_a[d], :, rows(c, 1 - d)]
        else:
            src = mix1.at[d, :, packed(c)]
        return copy(kind + d, c, src, got1.at[kind // 2, d, :, packed(c)], dev_a[d])

    def second(kind, c, d):
        if kind == F2:
            src = row16.at[far_b, rows(c, d)]
        elif kind == P2:
            src = row16.at[near_b[d], rows(c, 1 - d)]
        else:
            src = mix2.at[d, packed(c)]
        return copy(kind + d, c, src, got2.at[(kind - F2) // 2, d, packed(c)], dev_b[d])

    def along_z(c, d):
        here = hidden.at[feat, rows(c)]
        return copy(Z1 + d, c, here, here, dev_z[d])

    def relay_z(c, d):
        here = hidden.at[near_z[1 - d] * 2 + core, rows(c, d)]
        return copy(Z2 + d, c, here, here, dev_z[d])

    def to_mate(kind, c, which):
        f = ((z + which) % RING) * 2 + core
        here = hidden.at[f, rows(c)]
        return copy(kind, c, here, here, mate)

    def mate_copies(c):
        return [to_mate(OWN, c, 0), to_mate(FWD1, c, 1), to_mate(FWD1 + 1, c, 3), to_mate(FWD2, c, 2)]

    def send_far1(c):
        for d in (0, 1):
            first(F1, c, d).start()

    def send_plain1(c):
        for d in (0, 1):
            first(P1, c, d).start()

    def stage1(c):
        for d in (0, 1):
            first(F1, c, d).wait_recv()

            def add(jb, carry):
                mix1[d, jb, packed(c)] = (
                    part[near_a[d], jb, rows(c, d)].astype(jnp.float32)
                    + got1[0, d, jb, packed(c)].astype(jnp.float32)
                ).astype(jnp.bfloat16)
                return carry

            lax.fori_loop(0, RING, add, 0)
            first(C1, c, d).start()

    def stage2(c):
        for d in (0, 1):
            first(C1, c, d).wait_recv()
            first(P1, c, d).wait_recv()

        def add(jb, carry):
            for d in (0, 1):
                value = (
                    part[ia, jb, rows(c, d)].astype(jnp.float32)
                    + got1[1, d, jb, packed(c)].astype(jnp.float32)
                    + got1[2, 1 - d, jb, packed(c)].astype(jnp.float32)
                )
                row32[jb, rows(c, d)] = value
                row16[jb, rows(c, d)] = value.astype(jnp.bfloat16)
            return carry

        lax.fori_loop(0, RING, add, 0)
        for d in (0, 1):
            second(F2, c, d).start()
        for d in (0, 1):
            second(P2, c, d).start()

    def stage3(c):
        for d in (0, 1):
            second(F2, c, d).wait_recv()
            mix2[d, packed(c)] = (
                row32[near_b[d], rows(c, d)] + got2[0, d, packed(c)].astype(jnp.float32)
            ).astype(jnp.bfloat16)
            second(C2, c, d).start()

    def stage4(c):
        for d in (0, 1):
            second(C2, c, d).wait_recv()
            second(P2, c, d).wait_recv()
        for d in (0, 1):
            hidden[feat, rows(c, d)] = (
                row32[ib, rows(c, d)]
                + got2[1, d, packed(c)].astype(jnp.float32)
                + got2[2, 1 - d, packed(c)].astype(jnp.float32)
            ).astype(jnp.bfloat16)
        for d in (0, 1):
            along_z(c, d).start()
        to_mate(OWN, c, 0).start()

    def stage5(c):
        for d in (0, 1):
            along_z(c, d).wait_recv()
            relay_z(c, d).start()
        to_mate(FWD1, c, 1).start()
        to_mate(FWD1 + 1, c, 3).start()

    def stage6(c):
        for d in (0, 1):
            relay_z(c, d).wait_recv()
        to_mate(FWD2, c, 2).start()

    def stage7(c):
        for m in mate_copies(c):
            m.wait_recv()
        total = jnp.zeros((CHUNKS[c], BLOCK), jnp.float32)
        for f in range(2 * RING):
            total += jnp.dot(
                hidden[f, rows(c)],
                weight_ref[f * BLOCK : (f + 1) * BLOCK, :],
                preferred_element_type=jnp.float32,
            )
        out_ref[rows(c), :] = jnp.maximum(total, 0.0).astype(out_ref.dtype)

    n = len(CHUNKS)
    send_far1(0)
    send_plain1(0)
    send_far1(1)
    stages = (stage1, stage2, stage3, stage4, stage5, stage6, stage7)
    for t in range(n + len(stages) - 1):
        for lag, stage in enumerate(stages):
            c = t - lag
            if 0 <= c < n:
                stage(c)
            if lag == 0:
                if t + 1 < n:
                    send_plain1(t + 1)
                if t + 2 < n:
                    send_far1(t + 2)

    for c in range(n):
        for d in (0, 1):
            for kind in (F1, C1, P1):
                first(kind, c, d).wait_send()
            for kind in (F2, C2, P2):
                second(kind, c, d).wait_send()
            along_z(c, d).wait_send()
            relay_z(c, d).wait_send()
        for m in mate_copies(c):
            m.wait_send()


def exchange(part, weight):
    half = TGT_DEV // 2
    vmem = pl.BlockSpec(memory_space=pltpu.VMEM)
    return pl.pallas_call(
        exchange_kernel,
        out_shape=jax.ShapeDtypeStruct((TGT_DEV, BLOCK), jnp.bfloat16),
        in_specs=[vmem, vmem],
        out_specs=vmem,
        scratch_shapes=[
            pltpu.VMEM((3, 2, RING, half, BLOCK), jnp.bfloat16),
            pltpu.VMEM((2, RING, half, BLOCK), jnp.bfloat16),
            pltpu.VMEM((RING, TGT_DEV, BLOCK), jnp.float32),
            pltpu.VMEM((RING, TGT_DEV, BLOCK), jnp.bfloat16),
            pltpu.VMEM((3, 2, half, BLOCK), jnp.bfloat16),
            pltpu.VMEM((2, half, BLOCK), jnp.bfloat16),
            pltpu.VMEM((2 * RING, TGT_DEV, BLOCK), jnp.bfloat16),
            pltpu.SemaphoreType.DMA((KINDS, len(CHUNKS))),
            pltpu.SemaphoreType.DMA((KINDS, len(CHUNKS))),
        ],
        compiler_params=pltpu.CompilerParams(
            collective_id=0, has_side_effects=True, vmem_limit_bytes=32 << 20
        ),
        name="exchange",
    )(part, weight)


def body(sources, adjacency, target_block, source_block, slot_counts, weight):
    feat_width = sources.shape[1]
    blocks = sources.reshape(sources.shape[0] // BLOCK, BLOCK, feat_width)
    core = (lax.axis_index("feat") % 2).astype(jnp.int32).reshape(1)
    part = aggregate(core, target_block[0], source_block[0], slot_counts[0], adjacency[0], blocks)
    return exchange(part.reshape(RING, RING, TGT_DEV, feat_width), weight)


def solution(mesh):
    return jax.shard_map(
        body,
        mesh=mesh,
        in_specs=(
            P(("blk", "sub"), "feat"),
            P(("blk", "sub"), None, None, None, None),
            P(("blk", "sub"), None, None),
            P(("blk", "sub"), None, None),
            P(("blk", "sub"), None),
            P(None, "feat"),
        ),
        out_specs=P(("blk", "sub"), "feat"),
        check_vma=False,
    )
```

time: 164 us -> 75.4 us (0.46)
  waiting for transfers between devices: 123 us -> 0 us
  Pallas kernels: 14.7 us -> 70.6 us
  between operations: 13.4 us -> 0.03 us
  matrix products: 3 us -> 0 us
  local copies, waits for them, and re-layouts: 6.91 us -> 4.35 us
  other arithmetic: 1.77 us -> 0 us
    reduce_scatter x1 -> x0, waiting for transfers between devices: 94.9 us -> none  [body(): lax.psum_scatter(piece_terms.reshape(TGT_DEV * lax.axis_size(('blk', 'sub...]
    pallas_call x0 -> x1, Pallas kernels: none -> 56.6 us  [exchange(): pl.pallas_call(exchange_kernel, out_shape=jax.ShapeDtypeStruct((TGT_DEV,...]
    all_gather x1 -> x0, waiting for transfers between devices: 28.3 us -> none  [body(): lax.all_gather(hidden, 'feat', axis=1, tiled=True)]
    dot_general x1 -> x0, matrix products: 3 us -> none  [body(): jnp.dot(lax.all_gather(hidden, 'feat', axis=1, tiled=True), weight, prefe...]
    unnamed x12 -> x11, local copies, waits for them, and re-layouts: 6.91 us -> 4.35 us
    convert_element_type x1 -> x0, other arithmetic: 1.77 us -> none  [body(): hidden = summed.astype(jnp.bfloat16)]
  transfers between devices with their start and end apart: 2 -> 0, of which waited for: 2 -> 0; matrix products, arithmetic and copies ran while one was open for 0% -> 0% of each run, Pallas kernels for 0% -> 0%
where the time goes in v2:
time: 75.4 us; the launch traced here: 74.9 us
  Pallas kernels  70.6 us (94%)
  local copies, waits for them, and re-layouts  4.35 us (6%)
    pallas_call x1, Pallas kernels, exchange(): pl.pallas_call(exchange_kernel, out_shape=jax.ShapeDtypeStruct((TGT_DEV,...  56.6 us
    pallas_call x1, Pallas kernels, aggregate(): pl.pallas_call(aggregate_kernel, out_shape=jax.ShapeDtypeStruct((pieces,...  14 us
    unnamed x11, local copies, waits for them, and re-layouts  4.35 us

profile of v2, /device:TPU:1, one launch (start us, length us, event | category | flops | bytes accessed | tf_op | source)
XLA Modules:
  0.0 74.9 jit_solution(11588284115027655700)
XLA Ops:
  0.0 0.0 copy-start
  0.0 1.6 %copy-done = bf16[8192,128]{1,0:T(8,128)(2,1)S(1)} copy-done((bf16[8192,128]{1,0:T(8,128)(2,1)S(1)}, bf16[8192,128]{1,0:T(8,128)(2,1)}, u32[]{:S(2)}) %copy-start) | copy-done | bytes 2097176
  1.6 0.0 copy-start.2
  1.6 0.7 copy-done.2
  2.3 0.0 copy-start.3
  2.3 0.7 copy-done.3
  3.0 0.0 copy-start.4
  3.0 0.7 copy-done.4
  3.6 0.0 copy-start.1
  3.6 14.0 %aggregate.1 = bf16[16,1024,128]{2,1,0:T(8,128)(2,1)S(1)} custom-call(s32[1]{0:T(128)} %bitcast.core_ref, s32[16,32]{1,0:T(8,128)S(1)} %bitcast.9, s32[16,32]{1,0:T(8,128)S(1)} %bitcast.10, s32[16]{0:T(128)S(1)} %bitcast.11, bf16[16,32,128,128]{3,2,1,0:T(8,128)(2,1)} %bitcast.12, bf16[64,128,128]{2,1,0:T(8,128)(2,1)S(1)} %bitcast.8), custom_call_target="tpu_custom_call" | custom-call | tf_op jit(solution)/shard_map/aggregate/pallas_call | solution.py:49
  17.6 0.0 copy-done.1
  17.6 56.6 %exchange.1 = bf16[1024,128]{1,0:T(8,128)(2,1)S(1)} custom-call(bf16[4,4,1024,128]{3,2,1,0:T(8,128)(2,1)S(1)} %bitcast.7, bf16[1024,128]{1,0:T(8,128)(2,1)S(1)} %copy-done.1), custom_call_target="tpu_custom_call" | custom-call | tf_op jit(solution)/shard_map/exchange/pallas_call | solution.py:277
  74.2 0.7 copy.8
Async XLA Ops:
  0.0 1.6 %copy-start = (bf16[8192,128]{1,0:T(8,128)(2,1)S(1)}, bf16[8192,128]{1,0:T(8,128)(2,1)}, u32[]{:S(2)}) copy-start(bf16[8192,128]{1,0:T(8,128)(2,1)} %param.6) | copy-start | bytes 6291460
  1.6 0.7 copy-start.2
  2.3 0.7 copy-start.3
  3.0 0.7 copy-start.4
  3.6 14.0 %copy-start.1 = (bf16[1024,128]{1,0:T(8,128)(2,1)S(1)}, bf16[1024,128]{1,0:T(8,128)(2,1)}, u32[]{:S(2)}) copy-start(bf16[1024,128]{1,0:T(8,128)(2,1)} %weight_ref.1) | copy-start | bytes 786436

commit v3 on v0

v3 whole, which is shorter than its diff:
```python
import jax
import jax.numpy as jnp
from jax import lax
from jax.experimental import pallas as pl
from jax.experimental.pallas import tpu as pltpu
from jax.sharding import PartitionSpec as P

BLOCK = 128
TGT_DEV = 1024
SLOTS = 32
RING = 4
PIECES = RING * RING
TARGETS = TGT_DEV // BLOCK
UNROLL = 16
CHUNKS = (64,) * 8
DIRECT = (7,)
LAGS = (0, 2, 4, 6, 8, 9)
MESH = pl.DeviceIdType.MESH

F1, C1, P1, F2, C2, P2, ZNEAR = range(0, 14, 2)
ZFAR, OWN, FWD0, FWD1, FWD2 = range(14, 19)
KINDS = 19

ORDER, SOURCE, KEEP, LAST = 0, SLOTS, 2 * SLOTS, 3 * SLOTS


def slot_table(target, source, count_ref, table):
    shape = target.shape
    row = lax.broadcasted_iota(jnp.int32, shape, 0)
    lane = lax.broadcasted_iota(jnp.int32, shape, 1)
    count = jnp.zeros(shape, jnp.int32)
    for p in range(PIECES):
        count = jnp.where(row == p, count_ref[0, p], count)
    key = jnp.where(lane < count, target, TARGETS)
    unique = key * SLOTS + lane
    rank = jnp.zeros(shape, jnp.int32)
    earlier = jnp.zeros(shape, jnp.int32)
    upto = jnp.zeros(shape, jnp.int32)
    hit = jnp.zeros(shape, jnp.int32)
    for j in range(SLOTS):
        key_j = jnp.broadcast_to(key[:, j : j + 1], shape)
        rank += jnp.where(key_j * SLOTS + j < unique, 1, 0)
        earlier += jnp.where((key_j == key) & (lane > j), 1, 0)
        upto += jnp.where(key_j <= lane, 1, 0)
        hit += jnp.where(key_j == lane, 1, 0)
    keep = jnp.where(earlier > 0, 1, 0)
    order = jnp.zeros(shape, jnp.int32)
    source_of = jnp.zeros(shape, jnp.int32)
    keep_of = jnp.zeros(shape, jnp.int32)
    for k in range(SLOTS):
        here = jnp.broadcast_to(rank[:, k : k + 1], shape) == lane
        order = jnp.where(here, k, order)
        source_of = jnp.where(here, jnp.broadcast_to(source[:, k : k + 1], shape), source_of)
        keep_of = jnp.where(here, jnp.broadcast_to(keep[:, k : k + 1], shape), keep_of)
    table[:, ORDER : ORDER + SLOTS] = order
    table[:, SOURCE : SOURCE + SLOTS] = source_of
    table[:, KEEP : KEEP + SLOTS] = keep_of
    table[:, LAST : LAST + SLOTS] = jnp.where(hit > 0, upto - 1, SLOTS)


def layer_kernel(
    target_hbm, source_hbm, count_hbm, adj_hbm, blocks_hbm, weight_hbm, out_ref, *scratch
):
    (target_ref, source_ref, count_ref, table_ref, table, blocks, weight_ref, sums, part, got1, mix1,
     row32, row16, got2, mix2, gotd, hidden, load_sems, adj_sems, send_sems, recv_sems) = scratch[:21]
    tiles = scratch[21:]

    blk, sub, feat = lax.axis_index("blk"), lax.axis_index("sub"), lax.axis_index("feat")
    x, y = blk // 2, (blk % 2) * 2 + sub
    z, core = feat // 2, feat % 2
    ia = x * (1 - core) + y * core
    ib = y * (1 - core) + x * core

    def at(ja, jb, jz, jcore):
        px = ja * (1 - core) + jb * core
        py = jb * (1 - core) + ja * core
        return (px * 2 + py // 2, py % 2, jz * 2 + jcore)

    step = (1, RING - 1)
    near_a = [(ia + s) % RING for s in step]
    near_b = [(ib + s) % RING for s in step]
    near_z = [(z + s) % RING for s in step]
    far_a, far_b, far_z = (ia + 2) % RING, (ib + 2) % RING, (z + 2) % RING
    dev_a = [at(j, ib, z, core) for j in near_a]
    dev_b = [at(ia, j, z, core) for j in near_b]
    dev_z = [at(ia, ib, j, core) for j in near_z]
    dev_b_far = at(ia, far_b, z, core)
    dev_z_far = at(ia, ib, far_z, core)
    mate = (blk, sub, z * 2 + 1 - core)

    small = [
        pltpu.make_async_copy(target_hbm, target_ref, load_sems.at[0]),
        pltpu.make_async_copy(source_hbm, source_ref, load_sems.at[1]),
        pltpu.make_async_copy(count_hbm, count_ref, load_sems.at[2]),
    ]
    for load in small:
        load.start()
    quarter = blocks.shape[0] // 4
    block_loads = [
        pltpu.make_async_copy(
            blocks_hbm.at[pl.ds(q * quarter, quarter)], blocks.at[pl.ds(q * quarter, quarter)], load_sems.at[3 + q]
        )
        for q in range(4)
    ]
    for load in block_loads:
        load.start()
    places = [(ja, jb) for ja in (far_a, near_a[0], near_a[1], ia) for jb in (0, 1, 2, 3)]

    def number(ja, jb):
        return (ja * (1 - core) + jb * core) * RING + jb * (1 - core) + ja * core

    tile_loads = [
        pltpu.make_async_copy(adj_hbm.at[number(ja, jb)], tiles[i], adj_sems.at[i])
        for i, (ja, jb) in enumerate(places)
    ]
    for load in tile_loads:
        load.start()
    weight_load = pltpu.make_async_copy(weight_hbm, weight_ref, load_sems.at[7])
    weight_load.start()

    barrier = pltpu.get_barrier_semaphore()
    everyone = dev_a + dev_b + dev_z + [dev_b_far, dev_z_far, mate]
    for device in everyone:
        pl.semaphore_signal(barrier, inc=1, device_id=device, device_id_type=MESH)

    sums[SLOTS] = jnp.zeros((BLOCK, BLOCK), jnp.float32)
    for load in small:
        load.wait()
    slot_table(target_ref[...], source_ref[...], count_ref, table_ref)
    to_scalars = pltpu.make_async_copy(table_ref, table, load_sems.at[8])
    to_scalars.start()
    to_scalars.wait()
    for load in block_loads:
        load.wait()

    def compute(i):
        tile_loads[i].wait()
        ja, jb = places[i]
        p = number(ja, jb)

        def group(g, total):
            products = []
            for u in range(UNROLL):
                slot = g * UNROLL + u
                products.append(
                    jnp.dot(
                        tiles[i][table[p, ORDER + slot]],
                        blocks[table[p, SOURCE + slot]],
                        preferred_element_type=jnp.float32,
                    )
                )
            for u in range(UNROLL):
                slot = g * UNROLL + u
                total = total * table[p, KEEP + slot].astype(jnp.float32) + products[u]
                sums[slot] = total
            return total

        lax.fori_loop(0, SLOTS // UNROLL, group, jnp.zeros((BLOCK, BLOCK), jnp.float32))
        for t in range(TARGETS):
            value = sums[table[p, LAST + t]]
            if i < 12:
                part[ja, jb, t // 4, (t % 4) * BLOCK : (t % 4 + 1) * BLOCK] = value.astype(jnp.bfloat16)
            else:
                row32[jb, t // 4, (t % 4) * BLOCK : (t % 4 + 1) * BLOCK] = value

    starts = [sum(CHUNKS[:c]) for c in range(len(CHUNKS))]

    def rows(c):
        return pl.ds(starts[c], CHUNKS[c])

    def copy(kind, c, src, dst, device):
        return pltpu.make_async_remote_copy(
            src_ref=src,
            dst_ref=dst,
            send_sem=send_sems.at[kind, c],
            recv_sem=recv_sems.at[kind, c],
            device_id=device,
            device_id_type=MESH,
        )

    def far1(jb, d):
        return copy(F1 + d, jb, part.at[far_a, jb, d], got1.at[0, d, jb], dev_a[d])

    def first(kind, c, d):
        if kind == P1:
            src = part.at[near_a[d], :, 1 - d, rows(c)]
        else:
            src = mix1.at[d, :, rows(c)]
        return copy(kind + d, c, src, got1.at[kind // 2, d, :, rows(c)], dev_a[d])

    def second(kind, c, d):
        if kind == F2:
            src = row16.at[far_b, d, rows(c)]
        elif kind == P2:
            src = row16.at[near_b[d], 1 - d, rows(c)]
        else:
            src = mix2.at[d, rows(c)]
        return copy(kind + d, c, src, got2.at[(kind - F2) // 2, d, rows(c)], dev_b[d])

    def straight(c):
        return [
            copy(C2 + d, c, row16.at[near_b[d], :, rows(c)], gotd.at[d, :, rows(c)], dev_b[d]) for d in (0, 1)
        ] + [copy(F2, c, row16.at[far_b, :, rows(c)], gotd.at[2, :, rows(c)], dev_b_far)]

    def along_z(c):
        here = hidden.at[feat, :, rows(c)]
        return [copy(ZNEAR + d, c, here, here, dev_z[d]) for d in (0, 1)] + [copy(ZFAR, c, here, here, dev_z_far)]

    def to_mate(kind, c, chip):
        here = hidden.at[chip * 2 + core, :, rows(c)]
        return copy(kind, c, here, here, mate)

    def mate_copies(c):
        return [
            to_mate(OWN, c, z),
            to_mate(FWD0, c, near_z[0]),
            to_mate(FWD1, c, near_z[1]),
            to_mate(FWD2, c, far_z),
        ]

    def stage1(c):
        for d in (0, 1):
            for jb in range(RING):
                if c == 0:
                    far1(jb, d).wait_recv()

            def add(jb, carry):
                mix1[d, jb, rows(c)] = (
                    part[near_a[d], jb, d, rows(c)].astype(jnp.float32)
                    + got1[0, d, jb, rows(c)].astype(jnp.float32)
                ).astype(jnp.bfloat16)
                return carry

            lax.fori_loop(0, RING, add, 0)
            first(C1, c, d).start()
        for d in (0, 1):
            first(P1, c, d).start()

    def stage2(c):
        for d in (0, 1):
            first(C1, c, d).wait_recv()
            first(P1, c, d).wait_recv()

        def add(jb, carry):
            for d in (0, 1):
                value = (
                    row32[jb, d, rows(c)]
                    + got1[1, d, jb, rows(c)].astype(jnp.float32)
                    + got1[2, 1 - d, jb, rows(c)].astype(jnp.float32)
                )
                row32[jb, d, rows(c)] = value
                row16[jb, d, rows(c)] = value.astype(jnp.bfloat16)
            return carry

        lax.fori_loop(0, RING, add, 0)
        if c in DIRECT:
            for s in straight(c):
                s.start()
        else:
            for d in (0, 1):
                second(F2, c, d).start()
            for d in (0, 1):
                second(P2, c, d).start()

    def stage3(c):
        if c in DIRECT:
            return
        for d in (0, 1):
            second(F2, c, d).wait_recv()
            mix2[d, rows(c)] = (
                row32[near_b[d], d, rows(c)] + got2[0, d, rows(c)].astype(jnp.float32)
            ).astype(jnp.bfloat16)
            second(C2, c, d).start()

    def stage4(c):
        if c in DIRECT:
            for s in straight(c):
                s.wait_recv()
            for d in (0, 1):
                hidden[feat, d, rows(c)] = (
                    row32[ib, d, rows(c)]
                    + gotd[0, d, rows(c)].astype(jnp.float32)
                    + gotd[1, d, rows(c)].astype(jnp.float32)
                    + gotd[2, d, rows(c)].astype(jnp.float32)
                ).astype(jnp.bfloat16)
        else:
            for d in (0, 1):
                second(C2, c, d).wait_recv()
                second(P2, c, d).wait_recv()
            for d in (0, 1):
                hidden[feat, d, rows(c)] = (
                    row32[ib, d, rows(c)]
                    + got2[1, d, rows(c)].astype(jnp.float32)
                    + got2[2, 1 - d, rows(c)].astype(jnp.float32)
                ).astype(jnp.bfloat16)
        for s in along_z(c):
            s.start()
        to_mate(OWN, c, z).start()

    def stage5(c):
        for s, kind, chip in zip(along_z(c), (FWD1, FWD0, FWD2), (near_z[1], near_z[0], far_z)):
            s.wait_recv()
            to_mate(kind, c, chip).start()

    def stage6(c):
        if c == 0:
            weight_load.wait()
        for m in mate_copies(c):
            m.wait_recv()
        total = jnp.zeros((2 * CHUNKS[c], BLOCK), jnp.float32)
        for f in range(2 * RING):
            total += jnp.dot(
                hidden[f, :, rows(c)].reshape(2 * CHUNKS[c], BLOCK),
                weight_ref[f * BLOCK : (f + 1) * BLOCK, :],
                preferred_element_type=jnp.float32,
            )
        value = jnp.maximum(total, 0.0).astype(out_ref.dtype)
        for d in (0, 1):
            out_ref[d, rows(c)] = value[d * CHUNKS[c] : (d + 1) * CHUNKS[c]]

    n = len(CHUNKS)
    for i in range(PIECES):
        compute(i)
        if i == 0:
            pl.semaphore_wait(barrier, len(everyone))
        if i < RING:
            for d in (0, 1):
                far1(i, d).start()
    stages = (stage1, stage2, stage3, stage4, stage5, stage6)
    for t in range(n + LAGS[-1]):
        for lag, stage in zip(LAGS, stages):
            if 0 <= t - lag < n:
                stage(t - lag)

    for d in (0, 1):
        for jb in range(RING):
            far1(jb, d).wait_send()
    for c in range(n):
        for d in (0, 1):
            for kind in (C1, P1):
                first(kind, c, d).wait_send()
        if c in DIRECT:
            for s in straight(c):
                s.wait_send()
        else:
            for d in (0, 1):
                for kind in (F2, C2, P2):
                    second(kind, c, d).wait_send()
        for s in along_z(c) + mate_copies(c):
            s.wait_send()


def layer(target, source, count, adj, blocks, weight):
    half = TGT_DEV // 2
    n = len(CHUNKS)
    hbm = pl.BlockSpec(memory_space=pltpu.HBM)
    bf16, f32 = jnp.bfloat16, jnp.float32
    return pl.pallas_call(
        layer_kernel,
        out_shape=jax.ShapeDtypeStruct((2, half, BLOCK), bf16),
        in_specs=[hbm] * 6,
        out_specs=pl.BlockSpec(memory_space=pltpu.VMEM),
        scratch_shapes=[
            pltpu.VMEM(target.shape, jnp.int32),
            pltpu.VMEM(source.shape, jnp.int32),
            pltpu.SMEM(count.shape, jnp.int32),
            pltpu.VMEM((PIECES, 4 * SLOTS), jnp.int32),
            pltpu.SMEM((PIECES, 4 * SLOTS), jnp.int32),
            pltpu.VMEM(blocks.shape, bf16),
            pltpu.VMEM(weight.shape, bf16),
            pltpu.VMEM((SLOTS + 1, BLOCK, BLOCK), f32),
            pltpu.VMEM((RING, RING, 2, half, BLOCK), bf16),
            pltpu.VMEM((3, 2, RING, half, BLOCK), bf16),
            pltpu.VMEM((2, RING, half, BLOCK), bf16),
            pltpu.VMEM((RING, 2, half, BLOCK), f32),
            pltpu.VMEM((RING, 2, half, BLOCK), bf16),
            pltpu.VMEM((3, 2, half, BLOCK), bf16),
            pltpu.VMEM((2, half, BLOCK), bf16),
            pltpu.VMEM((3, 2, half, BLOCK), bf16),
            pltpu.VMEM((2 * RING, 2, half, BLOCK), bf16),
            pltpu.SemaphoreType.DMA((9,)),
            pltpu.SemaphoreType.DMA((PIECES,)),
            pltpu.SemaphoreType.DMA((KINDS, n)),
            pltpu.SemaphoreType.DMA((KINDS, n)),
        ]
        + [pltpu.VMEM(adj.shape[1:], bf16) for _ in range(PIECES)],
        compiler_params=pltpu.CompilerParams(
            collective_id=0, has_side_effects=True, vmem_limit_bytes=56 << 20
        ),
        name="layer",
    )(target, source, count, adj, blocks, weight).reshape(TGT_DEV, BLOCK)


def body(sources, adjacency, target_block, source_block, slot_counts, weight):
    blocks = sources.reshape(sources.shape[0] // BLOCK, BLOCK, sources.shape[1])
    return layer(target_block[0], source_block[0], slot_counts, adjacency[0], blocks, weight)


def solution(mesh):
    return jax.shard_map(
        body,
        mesh=mesh,
        in_specs=(
            P(("blk", "sub"), "feat"),
            P(("blk", "sub"), None, None, None, None),
            P(("blk", "sub"), None, None),
            P(("blk", "sub"), None, None),
            P(("blk", "sub"), None),
            P(None, "feat"),
        ),
        out_specs=P(("blk", "sub"), "feat"),
        check_vma=False,
    )
```

time: 232 us -> 56.6 us (0.24)
  waiting for transfers between devices: 116 us -> 0 us
  matrix products: 55.5 us -> 0 us
  Pallas kernels: 0 us -> 54.8 us
  local copies, waits for them, and re-layouts: 44.3 us -> 1.67 us
  between operations: 13.4 us -> 0.01 us
    reduce_scatter x1 -> x0, waiting for transfers between devices: 87.6 us -> none  [body(): lax.psum_scatter(piece_terms.reshape(TGT_DEV * lax.axis_size(('blk', 'sub...]
    dot_general x4 -> x0, matrix products: 55.5 us -> none  [the longest x1 23.3 us: one_piece(): jnp.einsum('sij,sjf->sif', adj_piece, selected, preferred_element_type=jn...]
    pallas_call x0 -> x1, Pallas kernels: none -> 54.8 us  [layer(): pl.pallas_call(layer_kernel, out_shape=jax.ShapeDtypeStruct((2, half, BLO...]
    dot_general x2 -> x0, local copies, waits for them, and re-layouts: 42.7 us -> none  [the longest x1 34.6 us: one_piece(): jnp.einsum('sij,sjf->sif', adj_piece, selected, preferred_element_type=jn...]
    all_gather x1 -> x0, waiting for transfers between devices: 28.5 us -> none  [body(): lax.all_gather(hidden, 'feat', axis=1, tiled=True)]
  transfers between devices with their start and end apart: 2 -> 0, of which waited for: 2 -> 0; matrix products, arithmetic and copies ran while one was open for 0% -> 0% of each run, Pallas kernels for 0% -> 0%
where the time goes in v3:
time: 56.6 us; the launch traced here: 56.5 us
  Pallas kernels  54.8 us (97%)
  local copies, waits for them, and re-layouts  1.67 us (3%)
    pallas_call x1, Pallas kernels, layer(): pl.pallas_call(layer_kernel, out_shape=jax.ShapeDtypeStruct((2, half, BLO...  54.8 us
    unnamed x1, local copies, waits for them, and re-layouts  1.67 us

profile of v3, /device:TPU:1, one launch (start us, length us, event | category | flops | bytes accessed | tf_op | source)
XLA Modules:
  0.0 56.5 jit_solution(7438104359071976892)
XLA Ops:
  0.0 54.8 %layer.1 = bf16[2,512,128]{2,1,0:T(8,128)(2,1)} custom-call(s32[16,32]{1,0:T(8,128)} %bitcast.8, s32[16,32]{1,0:T(8,128)} %bitcast.9, s32[1,16]{1,0:T(1,128)} %count_hbm.1, bf16[16,32,128,128]{3,2,1,0:T(8,128)(2,1)} %bitcast.5, bf16[64,128,128]{2,1,0:T(8,128)(2,1)} %bitcast.6, bf16[1024,128]{1,0:T(8,128)(2,1)} %weight_hbm.1), custom_call_target="tpu_custom_call" | custom-call | tf_op jit(solution)/shard_map/layer/pallas_call | solution.py:358
  54.8 1.7 %copy.8 = bf16[1024,128]{1,0:T(8,128)(2,1)} copy(bf16[1024,128]{1,0:T(8,128)(2,1)} %bitcast.7) | data formatting | bytes 524288

commit v4 on v3

--- a/solution.py
+++ b/solution.py
@@ -12,9 +12,12 @@
 PIECES = RING * RING
 TARGETS = TGT_DEV // BLOCK
 UNROLL = 16
-CHUNKS = (64,) * 8
-DIRECT = (7,)
-LAGS = (0, 2, 4, 6, 8, 9)
+CHUNKS = (160, 160, 128, 64)
+DIRECT = (0, 1, 2, 3)
+AHEAD = 2
+BOTH = (3,)
+VMEM_LIMIT = 56 << 20
+LAGS = (0, 4, 4, 5, 6, 7)
 MESH = pl.DeviceIdType.MESH
 
 F1, C1, P1, F2, C2, P2, ZNEAR = range(0, 14, 2)
@@ -86,6 +89,7 @@
     dev_z = [at(ia, ib, j, core) for j in near_z]
     dev_b_far = at(ia, far_b, z, core)
     dev_z_far = at(ia, ib, far_z, core)
+    dev_other = [at(ia, ib, j, 1 - core) for j in (near_z[0], near_z[1], far_z)]
     mate = (blk, sub, z * 2 + 1 - core)
 
     small = [
@@ -113,19 +117,18 @@
         pltpu.make_async_copy(adj_hbm.at[number(ja, jb)], tiles[i], adj_sems.at[i])
         for i, (ja, jb) in enumerate(places)
     ]
-    for load in tile_loads:
-        load.start()
     weight_load = pltpu.make_async_copy(weight_hbm, weight_ref, load_sems.at[7])
-    weight_load.start()
 
     barrier = pltpu.get_barrier_semaphore()
-    everyone = dev_a + dev_b + dev_z + [dev_b_far, dev_z_far, mate]
+    everyone = dev_a + dev_b + dev_z + [dev_b_far, dev_z_far, mate] + dev_other
     for device in everyone:
         pl.semaphore_signal(barrier, inc=1, device_id=device, device_id_type=MESH)
 
     sums[SLOTS] = jnp.zeros((BLOCK, BLOCK), jnp.float32)
     for load in small:
         load.wait()
+    for load in tile_loads + [weight_load]:
+        load.start()
     slot_table(target_ref[...], source_ref[...], count_ref, table_ref)
     to_scalars = pltpu.make_async_copy(table_ref, table, load_sems.at[8])
     to_scalars.start()
@@ -163,7 +166,8 @@
             else:
                 row32[jb, t // 4, (t % 4) * BLOCK : (t % 4 + 1) * BLOCK] = value
 
-    starts = [sum(CHUNKS[:c]) for c in range(len(CHUNKS))]
+    n = len(CHUNKS)
+    starts = [sum(CHUNKS[:c]) for c in range(n)]
 
     def rows(c):
         return pl.ds(starts[c], CHUNKS[c])
@@ -211,6 +215,11 @@
         return copy(kind, c, here, here, mate)
 
     def mate_copies(c):
+        if c in BOTH:
+            here = hidden.at[feat, :, rows(c)]
+            return [to_mate(OWN, c, z)] + [
+                copy(kind, c, here, here, device) for kind, device in zip((FWD0, FWD1, FWD2), dev_other)
+            ]
         return [
             to_mate(OWN, c, z),
             to_mate(FWD0, c, near_z[0]),
@@ -233,8 +242,9 @@
 
             lax.fori_loop(0, RING, add, 0)
             first(C1, c, d).start()
-        for d in (0, 1):
-            first(P1, c, d).start()
+        if c + AHEAD < n:
+            for d in (0, 1):
+                first(P1, c + AHEAD, d).start()
 
     def stage2(c):
         for d in (0, 1):
@@ -295,12 +305,14 @@
                 ).astype(jnp.bfloat16)
         for s in along_z(c):
             s.start()
-        to_mate(OWN, c, z).start()
+        for s in mate_copies(c) if c in BOTH else [to_mate(OWN, c, z)]:
+            s.start()
 
     def stage5(c):
         for s, kind, chip in zip(along_z(c), (FWD1, FWD0, FWD2), (near_z[1], near_z[0], far_z)):
             s.wait_recv()
-            to_mate(kind, c, chip).start()
+            if c not in BOTH:
+                to_mate(kind, c, chip).start()
 
     def stage6(c):
         if c == 0:
@@ -318,7 +330,6 @@
         for d in (0, 1):
             out_ref[d, rows(c)] = value[d * CHUNKS[c] : (d + 1) * CHUNKS[c]]
 
-    n = len(CHUNKS)
     for i in range(PIECES):
         compute(i)
         if i == 0:
@@ -326,6 +337,9 @@
         if i < RING:
             for d in (0, 1):
                 far1(i, d).start()
+        if i in (2 * RING - 1, 3 * RING - 1):
+            for c in range(AHEAD):
+                first(P1, c, i // RING - 1).start()
     stages = (stage1, stage2, stage3, stage4, stage5, stage6)
     for t in range(n + LAGS[-1]):
         for lag, stage in zip(LAGS, stages):
@@ -357,7 +371,7 @@
     bf16, f32 = jnp.bfloat16, jnp.float32
     return pl.pallas_call(
         layer_kernel,
-        out_shape=jax.ShapeDtypeStruct((2, half, BLOCK), bf16),
+        out_shape=pltpu.VMEM((2, half, BLOCK), bf16),
         in_specs=[hbm] * 6,
         out_specs=pl.BlockSpec(memory_space=pltpu.VMEM),
         scratch_shapes=[
@@ -385,7 +399,7 @@
         ]
         + [pltpu.VMEM(adj.shape[1:], bf16) for _ in range(PIECES)],
         compiler_params=pltpu.CompilerParams(
-            collective_id=0, has_side_effects=True, vmem_limit_bytes=56 << 20
+            collective_id=0, has_side_effects=True, vmem_limit_bytes=VMEM_LIMIT
         ),
         name="layer",
     )(target, source, count, adj, blocks, weight).reshape(TGT_DEV, BLOCK)

time: 56.6 us -> 47.1 us (0.83)
  Pallas kernels: 54.8 us -> 46.3 us
  local copies, waits for them, and re-layouts: 1.67 us -> 0.71 us
    pallas_call x1, Pallas kernels: 54.8 us -> 46.3 us  [layer(): pl.pallas_call(layer_kernel, out_shape=pltpu.VMEM((2, half, BLOCK), bf16)...]
    unnamed x1, local copies, waits for them, and re-layouts: 1.67 us -> 0.71 us
where the time goes in v4:
time: 47.1 us; the launch traced here: 47 us
  Pallas kernels  46.3 us (98%)
  local copies, waits for them, and re-layouts  0.71 us (2%)
    pallas_call x1, Pallas kernels, layer(): pl.pallas_call(layer_kernel, out_shape=pltpu.VMEM((2, half, BLOCK), bf16)...  46.3 us

profile of v4, /device:TPU:1, one launch (start us, length us, event | category | flops | bytes accessed | tf_op | source)
XLA Modules:
  0.0 47.0 jit_solution(12699178662979866923)
XLA Ops:
  0.0 46.3 %layer.1 = bf16[2,512,128]{2,1,0:T(8,128)(2,1)S(1)} custom-call(s32[16,32]{1,0:T(8,128)} %bitcast.8, s32[16,32]{1,0:T(8,128)} %bitcast.9, s32[1,16]{1,0:T(1,128)} %count_hbm.1, bf16[16,32,128,128]{3,2,1,0:T(8,128)(2,1)} %bitcast.6, bf16[64,128,128]{2,1,0:T(8,128)(2,1)} %bitcast.7, bf16[1024,128]{1,0:T(8,128)(2,1)} %weight_hbm.1), custom_call_target="tpu_custom_call" | custom-call | tf_op jit(solution)/shard_map/layer/pallas_call | solution.py:372
  46.3 0.7 %copy.8 = bf16[1024,128]{1,0:T(8,128)(2,1)} copy(bf16[1024,128]{1,0:T(8,128)(2,1)S(1)} %bitcast.5) | data formatting | bytes 524288

commit v5 on v4

--- a/solution.py
+++ b/solution.py
@@ -11,7 +11,7 @@
 RING = 4
 PIECES = RING * RING
 TARGETS = TGT_DEV // BLOCK
-UNROLL = 16
+UNROLL = 32
 CHUNKS = (160, 160, 128, 64)
 DIRECT = (0, 1, 2, 3)
 AHEAD = 2
@@ -117,6 +117,8 @@
         pltpu.make_async_copy(adj_hbm.at[number(ja, jb)], tiles[i], adj_sems.at[i])
         for i, (ja, jb) in enumerate(places)
     ]
+    for load in tile_loads[:1]:
+        load.start()
     weight_load = pltpu.make_async_copy(weight_hbm, weight_ref, load_sems.at[7])
 
     barrier = pltpu.get_barrier_semaphore()
@@ -127,7 +129,7 @@
     sums[SLOTS] = jnp.zeros((BLOCK, BLOCK), jnp.float32)
     for load in small:
         load.wait()
-    for load in tile_loads + [weight_load]:
+    for load in tile_loads[1:] + [weight_load]:
         load.start()
     slot_table(target_ref[...], source_ref[...], count_ref, table_ref)
     to_scalars = pltpu.make_async_copy(table_ref, table, load_sems.at[8])

time: 47.1 us -> 46.3 us (0.983)
  Pallas kernels: 46.3 us -> 45.5 us
    pallas_call x1, Pallas kernels: 46.3 us -> 45.5 us  [layer(): pl.pallas_call(layer_kernel, out_shape=pltpu.VMEM((2, half, BLOCK), bf16)...]
where the time goes in v5:
time: 46.3 us; the launch traced here: 46.2 us
  Pallas kernels  45.5 us (98%)
  local copies, waits for them, and re-layouts  0.71 us (2%)
    pallas_call x1, Pallas kernels, layer(): pl.pallas_call(layer_kernel, out_shape=pltpu.VMEM((2, half, BLOCK), bf16)...  45.5 us

profile of v5, /device:TPU:1, one launch (start us, length us, event | category | flops | bytes accessed | tf_op | source)
XLA Modules:
  0.0 46.2 jit_solution(15449915389301361567)
XLA Ops:
  0.0 45.5 %layer.1 = bf16[2,512,128]{2,1,0:T(8,128)(2,1)S(1)} custom-call(s32[16,32]{1,0:T(8,128)} %bitcast.8, s32[16,32]{1,0:T(8,128)} %bitcast.9, s32[1,16]{1,0:T(1,128)} %count_hbm.1, bf16[16,32,128,128]{3,2,1,0:T(8,128)(2,1)} %bitcast.6, bf16[64,128,128]{2,1,0:T(8,128)(2,1)} %bitcast.7, bf16[1024,128]{1,0:T(8,128)(2,1)} %weight_hbm.1), custom_call_target="tpu_custom_call" | custom-call | tf_op jit(solution)/shard_map/layer/pallas_call | solution.py:374
  45.5 0.7 %copy.8 = bf16[1024,128]{1,0:T(8,128)(2,1)} copy(bf16[1024,128]{1,0:T(8,128)(2,1)S(1)} %bitcast.5) | data formatting | bytes 524288

commit v6 on v5

--- a/solution.py
+++ b/solution.py
@@ -17,7 +17,7 @@
 AHEAD = 2
 BOTH = (3,)
 VMEM_LIMIT = 56 << 20
-LAGS = (0, 4, 4, 5, 6, 7)
+STEPS = ((2, 0), (2, 1), (4, 0), (2, 2), (4, 1), (2, 3), (5, 0), (4, 2), (6, 0), (5, 1), (4, 3), (6, 1), (5, 2), (6, 2), (5, 3), (6, 3))
 MESH = pl.DeviceIdType.MESH
 
 F1, C1, P1, F2, C2, P2, ZNEAR = range(0, 14, 2)
@@ -342,11 +342,11 @@
         if i in (2 * RING - 1, 3 * RING - 1):
             for c in range(AHEAD):
                 first(P1, c, i // RING - 1).start()
-    stages = (stage1, stage2, stage3, stage4, stage5, stage6)
-    for t in range(n + LAGS[-1]):
-        for lag, stage in zip(LAGS, stages):
-            if 0 <= t - lag < n:
-                stage(t - lag)
+    for c in range(n):
+        stage1(c)
+    stages = {2: stage2, 4: stage4, 5: stage5, 6: stage6}
+    for stage, c in STEPS:
+        stages[stage](c)
 
     for d in (0, 1):
         for jb in range(RING):

time: 46.3 us -> 46.3 us (level)
  no operation moved by 1% of the time
where the time goes in v6:
time: 46.3 us; the launch traced here: 46.2 us
  Pallas kernels  45.5 us (98%)
  local copies, waits for them, and re-layouts  0.71 us (2%)
    pallas_call x1, Pallas kernels, layer(): pl.pallas_call(layer_kernel, out_shape=pltpu.VMEM((2, half, BLOCK), bf16)...  45.5 us

profile of v6, /device:TPU:1, one launch (start us, length us, event | category | flops | bytes accessed | tf_op | source)
XLA Modules:
  0.0 46.2 jit_solution(15655406166306082079)
XLA Ops:
  0.0 45.5 %layer.1 = bf16[2,512,128]{2,1,0:T(8,128)(2,1)S(1)} custom-call(s32[16,32]{1,0:T(8,128)} %bitcast.8, s32[16,32]{1,0:T(8,128)} %bitcast.9, s32[1,16]{1,0:T(1,128)} %count_hbm.1, bf16[16,32,128,128]{3,2,1,0:T(8,128)(2,1)} %bitcast.6, bf16[64,128,128]{2,1,0:T(8,128)(2,1)} %bitcast.7, bf16[1024,128]{1,0:T(8,128)(2,1)} %weight_hbm.1), custom_call_target="tpu_custom_call" | custom-call | tf_op jit(solution)/shard_map/layer/pallas_call | solution.py:374
  45.5 0.7 %copy.8 = bf16[1024,128]{1,0:T(8,128)(2,1)} copy(bf16[1024,128]{1,0:T(8,128)(2,1)S(1)} %bitcast.5) | data formatting | bytes 524288
